TPU v7x, 32 devices: a whole 2x2x4 slice. The times are simulated.
32 devices in a mesh: dp: 16 (over z, x, core), head: 2 (over y).
Axes of the slice: x: 2, y: 2, z: 4, core: 2. Of those that a mesh axis runs over, the one named last changes fastest.
Arguments:
- layer_input: bfloat16 [16384, 1152], P(('dp', 'head')), may hold values from -6 to 6
- seq_lengths: int32 [16, 4], P('dp'), may hold values from 0 to 1024, as said below
- input_gain: float32 [1152], replicated, may hold values from -0.4 to 0.4
- query_weight: bfloat16 [1152, 1024], P(None, 'head'), may hold values from -0.1875 to 0.1875
- key_weight: bfloat16 [1152, 256], replicated, may hold values from -0.1875 to 0.1875
- value_weight: bfloat16 [1152, 256], replicated, may hold values from -0.1875 to 0.1875
- query_gain: float32 [256], replicated, may hold values from -0.4 to 0.4
- key_gain: float32 [256], replicated, may hold values from -0.4 to 0.4
- output_weight: bfloat16 [1152, 1024], P(None, 'head'), may hold values from -0.1875 to 0.1875
- post_attn_gain: float32 [1152], replicated, may hold values from -0.4 to 0.4
- pre_ffn_gain: float32 [1152], replicated, may hold values from -0.4 to 0.4
- gate_weight: bfloat16 [1152, 6912], P(None, 'head'), may hold values from -0.1875 to 0.1875
- up_weight: bfloat16 [1152, 6912], P(None, 'head'), may hold values from -0.1875 to 0.1875
- down_weight: bfloat16 [1152, 6912], P(None, 'head'), may hold values from -0.078125 to 0.078125
- post_ffn_gain: float32 [1152], replicated, may hold values from -0.4 to 0.4
- out_cotangent: bfloat16 [16384, 1152], P(('dp', 'head')), may hold values from -6 to 6
Outputs:
- layer_output: bfloat16 [16384, 1152], P(('dp', 'head'))
- input_grad: bfloat16 [16384, 1152], P(('dp', 'head'))
- input_gain_grad: float32 [1152], P('dp')
- query_weight_grad: float32 [1152, 1024], P('dp', 'head')
- key_weight_grad: float32 [1152, 256], P('dp')
- value_weight_grad: float32 [1152, 256], P('dp')
- query_gain_grad: float32 [256], P('dp')
- key_gain_grad: float32 [256], P('dp')
- output_weight_grad: float32 [1152, 1024], P('dp', 'head')
- post_attn_gain_grad: float32 [1152], P('dp')
- pre_ffn_gain_grad: float32 [1152], P('dp')
- gate_weight_grad: float32 [1152, 6912], P('dp', 'head')
- up_weight_grad: float32 [1152, 6912], P('dp', 'head')
- down_weight_grad: float32 [1152, 6912], P('dp', 'head')
- post_ffn_gain_grad: float32 [1152], P('dp')
Inputs may be any that keep to these rules, and one draw needn't show every extreme that they name: `seq_lengths`: row b lists bucket b's sequences in order, packed from its first token; they sum to at most 1024 and the rest of the bucket is padding; a length may be 0. In every draw some bucket holds a single sequence of 1024 tokens.
All inputs are finite; a program needn't handle non-finite values.
Results may differ from a plain program's by a relative error of at most 0.023.
Values may be sent and summed in bfloat16 or wider, within the bound.
No kernel may reach another device: no remote copies, remote signals or barrier semaphores. Data moves between devices by JAX's collectives and lax.ppermute only.
A program may use at most 256 MiB of HBM per device.

v0:
```python
import jax
import jax.numpy as jnp
from jax import lax
from jax.sharding import PartitionSpec as P

HD = 256


EPSILON = 1e-06
ROPE_BASE = 1000000.0
NEG_FILL = -1e30


def normed(values, gain_vec):
    return (
        values
        * lax.rsqrt(jnp.mean(values * values, axis=-1, keepdims=True) + EPSILON)
        * (1.0 + gain_vec)
    )


def rotary(values, cosine, sine_table):
    half_width = values.shape[-1] // 2
    first_half = values[..., :half_width]
    second_half = values[..., half_width:]
    return jnp.concatenate(
        [
            first_half * cosine - second_half * sine_table,
            second_half * cosine + first_half * sine_table,
        ],
        axis=-1,
    )


def angle_tables(position, head_dim):
    frequency = ROPE_BASE ** (-2.0 * jnp.arange(head_dim // 2, dtype=jnp.float32) / head_dim)
    angle_grid = position.astype(jnp.float32)[:, None] * frequency[None, :]
    return (jnp.cos(angle_grid), jnp.sin(angle_grid))


def seq_tables(bucket_lens, bucket_rows):
    slot_total = bucket_lens.shape[0]
    seq_ends = jnp.cumsum(bucket_lens)
    token_ids = jnp.arange(bucket_rows, dtype=jnp.int32)
    segment = jnp.sum((seq_ends[None, :] <= token_ids[:, None]).astype(jnp.int32), axis=1)
    slot_ids = jnp.arange(slot_total, dtype=jnp.int32)
    seq_begin = jnp.sum(
        jnp.where(slot_ids[None, :] < segment[:, None], bucket_lens[None, :], 0), axis=1
    )
    return (segment, token_ids - seq_begin, token_ids)


def gelu_gate(gate_pre, up_pre):
    return jax.nn.gelu(gate_pre, approximate=True) * up_pre


def row_dot(left, right):
    return jnp.einsum("tc,dc->td", left, right, preferred_element_type=jnp.float32)


def col_dot(left, right):
    return jnp.einsum("td,tc->dc", left, right, preferred_element_type=jnp.float32)


def on_device(
    layer_input,
    seq_lengths,
    input_gain,
    query_weight,
    key_weight,
    value_weight,
    query_gain,
    key_gain,
    output_weight,
    post_attn_gain,
    pre_ffn_gain,
    gate_weight,
    up_weight,
    down_weight,
    post_ffn_gain,
    out_cotangent,
):
    tok_dev = layer_input.shape[0]
    head_count = lax.axis_size("head")
    bucket_rows = tok_dev * head_count
    local_heads = query_weight.shape[1] // HD
    slot_total = seq_lengths.shape[1]
    segment, position, token_ids = seq_tables(seq_lengths[0], bucket_rows)
    cosine, sine_table = angle_tables(position, HD)
    block_rows = min(512, bucket_rows)
    block_count = bucket_rows // block_rows
    score_scale = HD ** (-0.5)

    def block_scores(q_low, k_low, first_row):
        query_ids = token_ids[first_row : first_row + block_rows]
        query_seg = segment[first_row : first_row + block_rows]
        visible = (token_ids[None, :] == query_ids[:, None]) | (
            token_ids[None, :] < query_ids[:, None]
        ) & (segment[None, :] == query_seg[:, None]) & (query_seg[:, None] < slot_total)
        scores = (
            jnp.einsum(
                "qhd,kd->hqk",
                q_low[first_row : first_row + block_rows],
                k_low,
                preferred_element_type=jnp.float32,
            )
            * score_scale
        )
        return jnp.where(visible[None], scores, NEG_FILL)

    input_f32 = layer_input.astype(jnp.float32)
    normed_local, input_pull = jax.vjp(normed, input_f32, input_gain)
    normed_in = lax.all_gather(normed_local.astype(jnp.bfloat16), "head", axis=0, tiled=True)
    q_raw = jnp.dot(normed_in, query_weight, preferred_element_type=jnp.float32)
    k_raw = jnp.dot(normed_in, key_weight, preferred_element_type=jnp.float32)
    v_raw = jnp.dot(normed_in, value_weight, preferred_element_type=jnp.float32)

    def query_path(raw_in, gain_vec):
        return rotary(normed(raw_in, gain_vec), cosine[:, None, :], sine_table[:, None, :])

    def key_path(raw_in, gain_vec):
        return rotary(normed(raw_in, gain_vec), cosine, sine_table)

    q_rot, query_pull = jax.vjp(query_path, q_raw.reshape(bucket_rows, local_heads, HD), query_gain)
    k_rot, key_pull = jax.vjp(key_path, k_raw, key_gain)
    q_low = q_rot.astype(jnp.bfloat16)
    k_low = k_rot.astype(jnp.bfloat16)
    v_low = v_raw.astype(jnp.bfloat16)
    out_blocks = []
    log_totals = []
    for block_idx in range(block_count):
        first_row = block_idx * block_rows
        scores = block_scores(q_low, k_low, first_row)
        row_max = jnp.max(scores, axis=-1, keepdims=True)
        exp_scores = jnp.exp(scores - row_max)
        row_total = jnp.sum(exp_scores, axis=-1, keepdims=True)
        prob_f32 = exp_scores / row_total
        log_totals.append(row_max + jnp.log(row_total))
        out_blocks.append(
            jnp.einsum(
                "hqk,kd->qhd",
                prob_f32.astype(jnp.bfloat16),
                v_low,
                preferred_element_type=jnp.float32,
            )
        )
    attn_out = (
        jnp.concatenate(out_blocks, axis=0)
        .reshape(bucket_rows, local_heads * HD)
        .astype(jnp.bfloat16)
    )
    attn_proj = lax.psum_scatter(
        row_dot(attn_out, output_weight), "head", scatter_dimension=0, tiled=True
    )
    attn_branch, post_attn_pull = jax.vjp(normed, attn_proj, post_attn_gain)
    hidden_state = input_f32 + attn_branch
    ffn_local, pre_ffn_pull = jax.vjp(normed, hidden_state, pre_ffn_gain)
    grad_out = out_cotangent.astype(jnp.float32)
    ffn_in = lax.all_gather(ffn_local.astype(jnp.bfloat16), "head", axis=0, tiled=True)
    gate_pre = jnp.dot(ffn_in, gate_weight, preferred_element_type=jnp.float32)
    up_pre = jnp.dot(ffn_in, up_weight, preferred_element_type=jnp.float32)
    hidden_f32, gelu_pull = jax.vjp(gelu_gate, gate_pre, up_pre)
    hidden = hidden_f32.astype(jnp.bfloat16)
    ffn_proj = lax.psum_scatter(
        row_dot(hidden, down_weight).astype(jnp.bfloat16), "head", scatter_dimension=0, tiled=True
    ).astype(jnp.float32)
    ffn_branch, post_ffn_pull = jax.vjp(normed, ffn_proj, post_ffn_gain)
    layer_output = (hidden_state + ffn_branch).astype(jnp.bfloat16)
    ffn_grad_local, grad_post_ffn = post_ffn_pull(grad_out)
    ffn_grad = lax.all_gather(ffn_grad_local.astype(jnp.bfloat16), "head", axis=0, tiled=True)
    hidden_grad = jnp.dot(ffn_grad, down_weight, preferred_element_type=jnp.float32)
    grad_down = col_dot(ffn_grad, hidden)
    gate_grad, up_grad = gelu_pull(hidden_grad)
    gate_grad_low = gate_grad.astype(jnp.bfloat16)
    up_grad_low = up_grad.astype(jnp.bfloat16)
    grad_gate = col_dot(ffn_in, gate_grad_low)
    grad_up = col_dot(ffn_in, up_grad_low)
    ffn_in_grad = lax.psum_scatter(
        row_dot(gate_grad_low, gate_weight) + row_dot(up_grad_low, up_weight),
        "head",
        scatter_dimension=0,
        tiled=True,
    )
    state_grad_norm, grad_pre_ffn = pre_ffn_pull(ffn_in_grad)
    state_grad = grad_out + state_grad_norm
    attn_grad_local, grad_post_attn = post_attn_pull(state_grad)
    attn_grad = lax.all_gather(attn_grad_local.astype(jnp.bfloat16), "head", axis=0, tiled=True)
    grad_output = col_dot(attn_grad, attn_out)
    heads_grad = (
        jnp.dot(attn_grad, output_weight, preferred_element_type=jnp.float32)
        .reshape(bucket_rows, local_heads, HD)
        .astype(jnp.bfloat16)
    )
    query_blocks = []
    key_grad_sum = jnp.zeros((bucket_rows, HD), jnp.float32)
    value_grad_sum = jnp.zeros((bucket_rows, HD), jnp.float32)
    for block_idx in range(block_count):
        first_row = block_idx * block_rows
        scores = block_scores(q_low, k_low, first_row)
        prob_f32 = jnp.exp(scores - log_totals[block_idx])
        prob_low = prob_f32.astype(jnp.bfloat16)
        heads_rows = heads_grad[first_row : first_row + block_rows]
        prob_grad = jnp.einsum("qhd,kd->hqk", heads_rows, v_low, preferred_element_type=jnp.float32)
        row_delta = jnp.sum(prob_f32 * prob_grad, axis=-1, keepdims=True)
        score_grad = (prob_f32 * (prob_grad - row_delta)).astype(jnp.bfloat16)
        query_blocks.append(
            jnp.einsum("hqk,kd->qhd", score_grad, k_low, preferred_element_type=jnp.float32)
            * score_scale
        )
        key_grad_sum = (
            key_grad_sum
            + jnp.einsum(
                "hqk,qhd->kd",
                score_grad,
                q_low[first_row : first_row + block_rows],
                preferred_element_type=jnp.float32,
            )
            * score_scale
        )
        value_grad_sum = value_grad_sum + jnp.einsum(
            "hqk,qhd->kd", prob_low, heads_rows, preferred_element_type=jnp.float32
        )
    query_raw_grad, grad_query_gain = query_pull(jnp.concatenate(query_blocks, axis=0))
    key_raw_grad, grad_key_gain = key_pull(key_grad_sum)
    query_grad_low = query_raw_grad.reshape(bucket_rows, local_heads * HD).astype(jnp.bfloat16)
    key_grad_low = key_raw_grad.astype(jnp.bfloat16)
    value_grad_low = value_grad_sum.astype(jnp.bfloat16)
    grad_query = col_dot(normed_in, query_grad_low)
    grad_key = col_dot(normed_in, key_grad_low)
    grad_value = col_dot(normed_in, value_grad_low)
    normed_grad = lax.psum_scatter(
        (
            row_dot(query_grad_low, query_weight)
            + row_dot(key_grad_low, key_weight)
            + row_dot(value_grad_low, value_weight)
        ).astype(jnp.bfloat16),
        "head",
        scatter_dimension=0,
        tiled=True,
    ).astype(jnp.float32)
    input_grad_norm, grad_in_gain = input_pull(normed_grad)
    input_grad = (state_grad + input_grad_norm).astype(jnp.bfloat16)
    shared = (
        lax.psum(grad_key.astype(jnp.bfloat16), "head").astype(jnp.float32),
        lax.psum(grad_value.astype(jnp.bfloat16), "head").astype(jnp.float32),
        lax.psum(grad_in_gain.astype(jnp.bfloat16), "head").astype(jnp.float32),
        lax.psum(grad_query_gain.astype(jnp.bfloat16), "head").astype(jnp.float32),
        lax.psum(grad_key_gain.astype(jnp.bfloat16), "head").astype(jnp.float32),
        lax.psum(grad_post_attn.astype(jnp.bfloat16), "head").astype(jnp.float32),
        lax.psum(grad_pre_ffn.astype(jnp.bfloat16), "head").astype(jnp.float32),
        lax.psum(grad_post_ffn.astype(jnp.bfloat16), "head").astype(jnp.float32),
    )
    every_part = (
        lax.psum_scatter(grad_query, "dp", scatter_dimension=0, tiled=True),
        lax.psum_scatter(grad_output, "dp", scatter_dimension=0, tiled=True),
        lax.psum_scatter(grad_gate, "dp", scatter_dimension=0, tiled=True),
        lax.psum_scatter(grad_up, "dp", scatter_dimension=0, tiled=True),
        lax.psum_scatter(grad_down, "dp", scatter_dimension=0, tiled=True),
        lax.psum_scatter(shared[0], "dp", scatter_dimension=0, tiled=True),
        lax.psum_scatter(shared[1], "dp", scatter_dimension=0, tiled=True),
        lax.psum_scatter(shared[2], "dp", scatter_dimension=0, tiled=True),
        lax.psum_scatter(shared[3], "dp", scatter_dimension=0, tiled=True),
        lax.psum_scatter(shared[4], "dp", scatter_dimension=0, tiled=True),
        lax.psum_scatter(shared[5], "dp", scatter_dimension=0, tiled=True),
        lax.psum_scatter(shared[6], "dp", scatter_dimension=0, tiled=True),
        lax.psum_scatter(shared[7], "dp", scatter_dimension=0, tiled=True),
    )
    (
        query_part,
        output_part,
        gate_part,
        up_part,
        down_part,
        key_part,
        value_part,
        in_gain_part,
        query_gain_part,
        key_gain_part,
        post_attn_part,
        pre_ffn_part,
        post_ffn_part,
    ) = every_part
    return (
        layer_output,
        input_grad,
        in_gain_part,
        query_part,
        key_part,
        value_part,
        query_gain_part,
        key_gain_part,
        output_part,
        post_attn_part,
        pre_ffn_part,
        gate_part,
        up_part,
        down_part,
        post_ffn_part,
    )


def solution(mesh):
    placed = (
        P(("dp", "head"), None),
        P("dp", None),
        P(),
        P(None, "head"),
        P(),
        P(),
        P(),
        P(),
        P(None, "head"),
        P(),
        P(),
        P(None, "head"),
        P(None, "head"),
        P(None, "head"),
        P(),
        P(("dp", "head"), None),
    )
    return jax.shard_map(
        on_device,
        mesh=mesh,
        in_specs=placed,
        out_specs=(
            P(("dp", "head"), None),
            P(("dp", "head"), None),
            P("dp"),
            P("dp", "head"),
            P("dp", None),
            P("dp", None),
            P("dp"),
            P("dp"),
            P("dp", "head"),
            P("dp"),
            P("dp"),
            P("dp", "head"),
            P("dp", "head"),
            P("dp", "head"),
            P("dp"),
        ),
        check_vma=False,
    )
```

profile of v0, /device:TPU:0, one launch (start us, length us, event | category | flops | bytes accessed | tf_op | source)
XLA Modules:
  0.0 1387.4 jit_solution(4991355585984457061)
XLA Ops:
  16.6 35.8 %all-gather.5.cloned.1.call-done = bf16[1024,1152]{1,0:T(8,128)(2,1)} async-done(((bf16[512,1152]{1,0:T(8,128)(2,1)}), bf16[1024,1152]{1,0:T(8,128)(2,1)}) %all-gather.5.cloned.1.call-update) | async-done | bytes 2359312 | tf_op jit(solution)/shard_map/all_gather | solution.py:113
  81.5 3.7 fusion.102
  86.0 59.5 %reduce-scatter.18.cloned.1.call-done = f32[512,1152]{1,0:T(8,128)} async-done(((f32[1024,1152]{1,0:T(8,128)}), f32[512,1152]{1,0:T(8,128)}) %reduce-scatter.18.cloned.1.call-update) | async-done | bytes 2359312 | tf_op jit(solution)/shard_map/reduce_scatter | solution.py:152
  152.7 36.2 %all-gather.7.cloned.1.call-done = bf16[1024,1152]{1,0:T(8,128)(2,1)} async-done(((bf16[512,1152]{1,0:T(8,128)(2,1)}), bf16[1024,1152]{1,0:T(8,128)(2,1)}) %all-gather.7.cloned.1.call-update) | async-done | bytes 2359312 | tf_op jit(solution)/shard_map/all_gather | solution.py:159
  188.9 16.9 %fusion.103 = f32[1024,3456]{1,0:T(8,128)} fusion(bf16[1024,1152]{1,0:T(8,128)(2,1)} %all-gather.7.cloned.1.call-done, bf16[1152,3456]{1,0:T(8,128)(2,1)} %param.27), kind=kOutput, calls=%fused_computation.203 | convolution fusion | flops 8153726976 | bytes 24477696 | tf_op jit(solution)/shard_map/dot_general | solution.py:160
  205.9 20.1 %multiply_convert_fusion.1 = (bf16[1024,3456]{1,0:T(8,128)(2,1)}, f32[1024,3456]{1,0:T(8,128)}) fusion(f32[1024,3456]{1,0:T(8,128)} %fusion.103, bf16[1024,1152]{1,0:T(8,128)(2,1)S(1)} %copy-done.91, bf16[1152,3456]{1,0:T(8,128)(2,1)} %param.28), kind=kOutput, calls=%fused_computation.10 | convolution fusion | flops 8189116416 | bytes 45711360 | tf_op jit(solution)/shard_map/dot_general | solution.py:161
  226.0 15.0 %convolution_convert_fusion = bf16[1024,1152]{1,0:T(8,128)(2,1)} fusion(bf16[1024,3456]{1,0:T(8,128)(2,1)} %get-tuple-element.73, bf16[1152,3456]{1,0:T(8,128)(2,1)} %param.29), kind=kOutput, calls=%fused_computation.42 | convolution fusion | flops 8154906624 | bytes 17399808 | tf_op jit(solution)/shard_map/tc,dc->td/dot_general | solution.py:58
  242.4 33.5 %reduce-scatter.20.cloned.1.call-done = bf16[512,1152]{1,0:T(8,128)(2,1)} async-done(((bf16[1024,1152]{1,0:T(8,128)(2,1)}), bf16[512,1152]{1,0:T(8,128)(2,1)}) %reduce-scatter.20.cloned.1.call-update) | async-done | bytes 1179664 | tf_op jit(solution)/shard_map/reduce_scatter | solution.py:164
  282.6 36.2 %all-gather.9.cloned.1.call-done = bf16[1024,1152]{1,0:T(8,128)(2,1)} async-done(((bf16[512,1152]{1,0:T(8,128)(2,1)}), bf16[1024,1152]{1,0:T(8,128)(2,1)}) %all-gather.9.cloned.1.call-update) | async-done | bytes 2359312 | tf_op jit(solution)/shard_map/all_gather | solution.py:170
  318.8 25.3 %multiply_convert_fusion = (bf16[1024,3456]{1,0:T(8,128)(2,1)}, bf16[1024,3456]{1,0:T(8,128)(2,1)S(1)}) fusion(f32[1024,3456]{1,0:T(8,128)} %fusion.103, f32[1024,3456]{1,0:T(8,128)} %get-tuple-element.74, bf16[1024,1152]{1,0:T(8,128)(2,1)} %all-gather.9.cloned.1.call-done, bf16[1152,3456]{1,0:T(8,128)(2,1)} %param.29), kind=kOutput, calls=%fused_computation.9 | convolution fusion | flops 8238661632 | bytes 52789248 | tf_op jit(solution)/shard_map/dot_general | solution.py:171
  344.1 17.1 %fusion.104 = f32[1024,1152]{1,0:T(8,128)} fusion(bf16[1024,3456]{1,0:T(8,128)(2,1)S(1)} %get-tuple-element.45, bf16[1152,3456]{1,0:T(8,128)(2,1)} %param.27), kind=kOutput, calls=%fused_computation.204 | convolution fusion | flops 8153726976 | bytes 19759104 | tf_op jit(solution)/shard_map/tc,dc->td/dot_general | solution.py:58
  361.2 16.3 %convolution_add_fusion.2 = f32[1024,1152]{1,0:T(8,128)} fusion(f32[1024,1152]{1,0:T(8,128)} %fusion.104, bf16[1024,3456]{1,0:T(8,128)(2,1)} %get-tuple-element.44, bf16[1152,3456]{1,0:T(8,128)(2,1)} %param.28), kind=kOutput, calls=%fused_computation.19 | convolution fusion | flops 8154906624 | bytes 24477696 | tf_op jit(solution)/shard_map/tc,dc->td/dot_general | solution.py:58
  377.6 60.1 %reduce-scatter.22.cloned.1.call-done = f32[512,1152]{1,0:T(8,128)} async-done(((f32[1024,1152]{1,0:T(8,128)}), f32[512,1152]{1,0:T(8,128)}) %reduce-scatter.22.cloned.1.call-update) | async-done | bytes 2359312 | tf_op jit(solution)/shard_map/reduce_scatter | solution.py:178
  437.8 3.7 multiply_reduce_fusion
  441.6 4.8 multiply_reduce_fusion.1
  450.8 34.8 %all-gather.11.cloned.1.call-done = bf16[1024,1152]{1,0:T(8,128)(2,1)} async-done(((bf16[512,1152]{1,0:T(8,128)(2,1)}), bf16[1024,1152]{1,0:T(8,128)(2,1)}) %all-gather.11.cloned.1.call-update) | async-done | bytes 2359312 | tf_op jit(solution)/shard_map/all_gather | solution.py:187
  485.6 3.7 convolution_convert_fusion.3
  510.0 3.5 convolution_convert_fusion.1
  521.8 36.7 %all-reduce.18.cloned.1.call-done = (bf16[1152,256]{1,0:T(8,128)(2,1)}, bf16[1152,256]{1,0:T(8,128)(2,1)}) async-done(((bf16[1152,256]{1,0:T(8,128)(2,1)}, bf16[1152,256]{1,0:T(8,128)(2,1)}), (bf16[1152,256]{1,0:T(8,128)(2,1)}, bf16[1152,256]{1,0:T(8,128)(2,1)})) %all-reduce.18.cloned.1.call-update) | async-done | bytes 1179664 | tf_op jit(solution)/shard_map/psum | solution.py:244
  563.0 4.8 fusion.107
  567.8 4.1 fusion.106
  573.6 14.7 %fusion.110 = f32[1152,3456]{1,0:T(8,128)} fusion(bf16[1024,1152]{1,0:T(8,128)(2,1)S(1)} %copy-done.93, bf16[1024,3456]{1,0:T(8,128)(2,1)} %get-tuple-element.73), kind=kOutput, calls=%fused_computation.210 | convolution fusion | flops 8153726976 | bytes 25362432 | tf_op jit(solution)/shard_map/td,tc->dc/dot_general | solution.py:62
  590.0 14.6 %fusion.109 = f32[1152,3456]{1,0:T(8,128)} fusion(bf16[1024,1152]{1,0:T(8,128)(2,1)S(1)} %copy-done.92, bf16[1024,3456]{1,0:T(8,128)(2,1)} %get-tuple-element.44), kind=kOutput, calls=%fused_computation.209 | convolution fusion | flops 8153726976 | bytes 25362432 | tf_op jit(solution)/shard_map/td,tc->dc/dot_general | solution.py:62
  604.7 14.7 %fusion.108 = f32[1152,3456]{1,0:T(8,128)} fusion(bf16[1024,1152]{1,0:T(8,128)(2,1)S(1)} %copy-done.92, bf16[1024,3456]{1,0:T(8,128)(2,1)} %copy-done.96), kind=kOutput, calls=%fused_computation.208 | convolution fusion | flops 8153726976 | bytes 25362432 | tf_op jit(solution)/shard_map/td,tc->dc/dot_general | solution.py:62
  625.0 8.6 all-reduce.14
  633.6 61.6 %all-reduce.13 = (f32[1152]{0:T(1024)}, f32[256]{0:T(256)}, f32[256]{0:T(256)}, f32[1152]{0:T(1024)}, f32[1152]{0:T(1024)}, /*index=5*/f32[1152]{0:T(1024)}) all-reduce(bf16[1152]{0:T(1024)(128)(2,1)} %get-tuple-element.33, bf16[256]{0:T(256)(128)(2,1)} %get-tuple-element.34, ...), channel_id=6, replica_groups=mesh['dp'=16,'head'=2] {'dp'}, use_global_device_ids=true, to_apply=%region_27.28.clone | all-reduce | flops 5120 | bytes 30720
  706.8 12.9 reduce-scatter.30.cloned.1.call-done
  719.7 66.7 %reduce-scatter.32.cloned.1.call-done = f32[72,512]{1,0:T(8,128)} async-done(((f32[1152,512]{1,0:T(8,128)}), f32[72,512]{1,0:T(8,128)}) %reduce-scatter.32.cloned.1.call-update) | async-done | bytes 147472 | tf_op jit(solution)/shard_map/reduce_scatter | solution.py:255
  786.3 66.4 %reduce-scatter.26.cloned.1.call-done = f32[72,512]{1,0:T(8,128)} async-done(((f32[1152,512]{1,0:T(8,128)}), f32[72,512]{1,0:T(8,128)}) %reduce-scatter.26.cloned.1.call-update) | async-done | bytes 147472 | tf_op jit(solution)/shard_map/reduce_scatter | solution.py:254
  852.7 176.0 %reduce-scatter.38.cloned.1.call-done = f32[72,3456]{1,0:T(8,128)} async-done(((f32[1152,3456]{1,0:T(8,128)}), f32[72,3456]{1,0:T(8,128)}) %reduce-scatter.38.cloned.1.call-update) | async-done | bytes 995344
  1028.7 176.0 %reduce-scatter.36.cloned.1.call-done = f32[72,3456]{1,0:T(8,128)} async-done(((f32[1152,3456]{1,0:T(8,128)}), f32[72,3456]{1,0:T(8,128)}) %reduce-scatter.36.cloned.1.call-update) | async-done | bytes 995344
  1204.7 176.0 %reduce-scatter.34.cloned.1.call-done = f32[72,3456]{1,0:T(8,128)} async-done(((f32[1152,3456]{1,0:T(8,128)}), f32[72,3456]{1,0:T(8,128)}) %reduce-scatter.34.cloned.1.call-update) | async-done | bytes 995344
  (318 shorter events, 110.8 us)
Async XLA Ops:
  7.2 55.9 %copy-start = (bf16[1152,512]{1,0:T(8,128)(2,1)S(1)}, bf16[1152,512]{1,0:T(8,128)(2,1)}, u32[]{:S(2)}) copy-start(bf16[1152,512]{1,0:T(8,128)(2,1)} %param.19) | copy-start | bytes 3538948
  7.2 6.4 copy-start.90
  7.2 6.8 copy-start.88
  7.2 6.8 copy-start.89
  7.2 45.3 %all-gather.5.cloned.1.call-start = ((), (), s32[]{:S(2)}) async-start(), calls=%async_computation.11 | async-start | bytes 3538944 | tf_op jit(solution)/shard_map/all_gather | solution.py:113
  9.5 43.0 %copy-start.27 = (bf16[1152,256]{1,0:T(8,128)(2,1)S(1)}, bf16[1152,256]{1,0:T(8,128)(2,1)}, u32[]{:S(2)}) copy-start(bf16[1152,256]{1,0:T(8,128)(2,1)} %param.20) | copy-start | bytes 1769476
  13.5 131.9 %reduce-scatter.18.cloned.1.call-start = ((), (), s32[]{:S(2)}) async-start(), calls=%async_computation.12 | async-start | bytes 7077888 | tf_op jit(solution)/shard_map/reduce_scatter | solution.py:152
  13.8 42.0 %copy-start.86 = (f32[128]{0:T(128)}, f32[128]{0:T(128)S(1)}, u32[]{:S(2)}) copy-start(f32[128]{0:T(128)S(1)} %multiply_power_fusion) | copy-start | bytes 1540
  14.0 54.2 %copy-start.82 = (f32[256]{0:T(256)}, f32[256]{0:T(256)S(1)}, u32[]{:S(2)}) copy-start(f32[256]{0:T(256)S(1)} %broadcast_add_fusion.4) | copy-start | bytes 3076
  14.1 41.0 %copy-start.74 = (f32[256]{0:T(256)}, f32[256]{0:T(256)S(1)}, u32[]{:S(2)}) copy-start(f32[256]{0:T(256)S(1)} %broadcast_add_fusion.5) | copy-start | bytes 3076
  14.1 41.7 %copy-start.54 = (f32[1024]{0:T(1024)}, f32[1024]{0:T(1024)S(1)}, u32[]{:S(2)}) copy-start(f32[1024]{0:T(1024)S(1)} %subtract_convert_fusion.1) | copy-start | bytes 12292
  55.9 7.2 copy-start.29
  73.8 5.6 copy-start.1
  73.8 5.6 copy-start.78
  85.3 103.7 %all-gather.7.cloned.1.call-start = ((), (), s32[]{:S(2)}) async-start(), calls=%async_computation.13 | async-start | bytes 3538944 | tf_op jit(solution)/shard_map/all_gather | solution.py:159
  152.7 123.2 %reduce-scatter.20.cloned.1.call-start = ((), (), s32[]{:S(2)}) async-start(), calls=%async_computation.14 | async-start | bytes 3538944 | tf_op jit(solution)/shard_map/reduce_scatter | solution.py:164
  188.9 16.9 %copy-start.91 = (bf16[1024,1152]{1,0:T(8,128)(2,1)S(1)}, bf16[1024,1152]{1,0:T(8,128)(2,1)}, u32[]{:S(2)}) copy-start(bf16[1024,1152]{1,0:T(8,128)(2,1)} %all-gather.7.cloned.1.call-done) | copy-start | bytes 7077892
  241.0 77.8 %all-gather.9.cloned.1.call-start = ((), (), s32[]{:S(2)}) async-start(), calls=%async_computation.15 | async-start | bytes 3538944 | tf_op jit(solution)/shard_map/all_gather | solution.py:170
  282.6 155.1 %reduce-scatter.22.cloned.1.call-start = ((), (), s32[]{:S(2)}) async-start(), calls=%async_computation.16 | async-start | bytes 7077888 | tf_op jit(solution)/shard_map/reduce_scatter | solution.py:178
  344.1 17.1 %copy-start.96 = (bf16[1024,3456]{1,0:T(8,128)(2,1)}, bf16[1024,3456]{1,0:T(8,128)(2,1)S(1)}, u32[]{:S(2)}) copy-start(bf16[1024,3456]{1,0:T(8,128)(2,1)S(1)} %get-tuple-element.45) | copy-start | bytes 21233668
  377.6 108.0 %all-gather.11.cloned.1.call-start = ((), (), s32[]{:S(2)}) async-start(), calls=%async_computation.17 | async-start | bytes 3538944 | tf_op jit(solution)/shard_map/all_gather | solution.py:187
  449.4 109.1 %all-reduce.18.cloned.1.call-start = ((), (), s32[]{:S(2)}) async-start(), calls=%async_computation.26 | async-start | bytes 2359296 | tf_op jit(solution)/shard_map/psum | solution.py:244
  515.2 106.7 %reduce-scatter.24.cloned.1.call-start = ((), (), s32[]{:S(2)}) async-start(), calls=%async_computation.18 | async-start | bytes 3538944 | tf_op jit(solution)/shard_map/reduce_scatter | solution.py:231
  521.8 185.0 %reduce-scatter.28.cloned.1.call-start = ((), (), s32[]{:S(2)}) async-start(), calls=%async_computation.20 | async-start | bytes 1253376 | tf_op jit(solution)/shard_map/reduce_scatter | solution.py:259
  560.7 159.0 %reduce-scatter.30.cloned.1.call-start = ((), (), s32[]{:S(2)}) async-start(), calls=%async_computation.21 | async-start | bytes 1253376 | tf_op jit(solution)/shard_map/reduce_scatter | solution.py:260
  562.9 223.4 %reduce-scatter.32.cloned.1.call-start = ((), (), s32[]{:S(2)}) async-start(), calls=%async_computation.22 | async-start | bytes 2506752 | tf_op jit(solution)/shard_map/reduce_scatter | solution.py:255
  567.7 285.0 %reduce-scatter.26.cloned.1.call-start = ((), (), s32[]{:S(2)}) async-start(), calls=%async_computation.19 | async-start | bytes 2506752 | tf_op jit(solution)/shard_map/reduce_scatter | solution.py:254
  571.9 456.8 %reduce-scatter.38.cloned.1.call-start = ((), (), s32[]{:S(2)}) async-start(), calls=%async_computation.25 | async-start | bytes 16920576
  588.3 616.4 %reduce-scatter.36.cloned.1.call-start = ((), (), s32[]{:S(2)}) async-start(), calls=%async_computation.24 | async-start | bytes 16920576
  604.6 776.1 %reduce-scatter.34.cloned.1.call-start = ((), (), s32[]{:S(2)}) async-start(), calls=%async_computation.23 | async-start | bytes 16920576
  619.4 83.3 %copy-start.71 = (f32[512]{0:T(512)S(1)}, f32[512]{0:T(512)}, u32[]{:S(2)}) copy-start(f32[512]{0:T(512)} %copy-done.70) | copy-start | bytes 6148
  622.0 81.4 %copy-start.18 = (bf16[512,1152]{1,0:T(8,128)(2,1)S(1)}, bf16[512,1152]{1,0:T(8,128)(2,1)}, u32[]{:S(2)}) copy-start(bf16[512,1152]{1,0:T(8,128)(2,1)} %reduce-scatter.24.cloned.1.call-done) | copy-start | bytes 3538948
  (81 other events, 185.9 us)
Sparse Core Ops, SparseCore 0:
  13.7 38.7 all-gather.4
  85.4 59.9 reduce-scatter.17
  152.8 36.0 all-gather.6
  241.2 34.6 reduce-scatter.19
  282.7 36.0 all-gather.8
  377.7 59.9 reduce-scatter.21
  449.5 36.0 all-gather.10
  515.4 43.0 all-reduce.17
  560.7 34.7 reduce-scatter.23
  599.9 57.9 reduce-scatter.27
  662.6 57.0 reduce-scatter.29
  724.3 61.9 reduce-scatter.31
  790.7 62.0 reduce-scatter.25
  857.9 170.8 reduce-scatter.37
  1033.8 170.8 reduce-scatter.35
  1209.8 170.8 reduce-scatter.33
where the time goes:
time: 1390 us
  waiting for transfers between devices  1010 us (73%)
  matrix products  200 us (14%)
  blocking collectives  70.2 us (5%)
  other arithmetic  57.8 us (4%)
  local copies, waits for them, and re-layouts  34.9 us (3%)
  between operations  16.6 us (1%)
    unnamed x19, waiting for transfers between devices  528 us
    reduce_scatter x1, waiting for transfers between devices, on_device(): lax.psum_scatter(grad_output, 'dp', scatter_dimension=0, tiled=True)  66.7 us
    reduce_scatter x1, waiting for transfers between devices, on_device(): lax.psum_scatter(grad_query, 'dp', scatter_dimension=0, tiled=True)  66.4 us
    unnamed x1, blocking collectives  61.6 us
    reduce_scatter x1, waiting for transfers between devices, on_device(): lax.psum_scatter(row_dot(gate_grad_low, gate_weight) + row_dot(up_grad_lo...  60.1 us
    reduce_scatter x1, waiting for transfers between devices, on_device(): lax.psum_scatter(row_dot(attn_out, output_weight), 'head', scatter_dimens...  59.5 us
    dot_general x7, matrix products, row_dot(): jnp.einsum('tc,dc->td', left, right, preferred_element_type=jnp.float32)  58.3 us
    dot_general x7, matrix products, col_dot(): jnp.einsum('td,tc->dc', left, right, preferred_element_type=jnp.float32)  58.1 us
  transfers between devices with their start and end apart: 16, of which 14 were waited for; matrix products, arithmetic and copies ran while one was open for 6% of the time, Pallas kernels for 0%

commit v1 on v0

v1 whole, which is shorter than its diff:
```python
import jax
import jax.numpy as jnp
from jax import lax
from jax.sharding import PartitionSpec as P

HD = 256
EPSILON = 1e-06
ROPE_BASE = 1000000.0
NEG_FILL = -1e30
LOW = jnp.bfloat16
F32 = jnp.float32


def normed(values, gain_vec):
    return (
        values
        * lax.rsqrt(jnp.mean(values * values, axis=-1, keepdims=True) + EPSILON)
        * (1.0 + gain_vec)
    )


def rotary(values, cosine, sine_table):
    half_width = values.shape[-1] // 2
    first_half = values[..., :half_width]
    second_half = values[..., half_width:]
    return jnp.concatenate(
        [
            first_half * cosine - second_half * sine_table,
            second_half * cosine + first_half * sine_table,
        ],
        axis=-1,
    )


def angle_tables(position, head_dim):
    frequency = ROPE_BASE ** (-2.0 * jnp.arange(head_dim // 2, dtype=F32) / head_dim)
    angle_grid = position.astype(F32)[:, None] * frequency[None, :]
    return (jnp.cos(angle_grid), jnp.sin(angle_grid))


def seq_tables(bucket_lens, token_ids):
    seq_ends = jnp.cumsum(bucket_lens)
    segment = jnp.sum((seq_ends[None, :] <= token_ids[:, None]).astype(jnp.int32), axis=1)
    slot_ids = jnp.arange(bucket_lens.shape[0], dtype=jnp.int32)
    seq_begin = jnp.sum(
        jnp.where(slot_ids[None, :] < segment[:, None], bucket_lens[None, :], 0), axis=1
    )
    return segment, token_ids - seq_begin


def gelu_gate(gate_pre, up_pre):
    return jax.nn.gelu(gate_pre, approximate=True) * up_pre


def dot(left, right):
    return jnp.dot(left, right, preferred_element_type=F32)


def row_dot(left, right):
    return jnp.einsum("tc,dc->td", left, right, preferred_element_type=F32)


def col_dot(left, right):
    return jnp.einsum("td,tc->dc", left, right, preferred_element_type=F32)


def swap_head(value):
    return lax.ppermute(value, "head", [(0, 1), (1, 0)])


def pair(axis_size, bit):
    return [(i, i ^ (1 << bit)) for i in range(axis_size)]


def scatter_bits(parts, bits, axis_size, index, low=LOW):
    count = axis_size.bit_length() - 1
    rows = parts[0].shape[0] // axis_size
    parts = [p.reshape((2,) * count + (rows,) + p.shape[1:]) for p in parts]
    left = list(range(count - 1, -1, -1))

    def take(p, dim, which):
        return lax.dynamic_index_in_dim(p, which, axis=dim, keepdims=False)

    for bit in bits:
        dim = left.index(bit)
        mine = (index >> bit) & 1
        send = sum(take(p, dim, 1 - mine).astype(F32) for p in parts).astype(low)
        got = lax.ppermute(send, "dp", pair(axis_size, bit))
        parts = [take(p, dim, mine) for p in parts] + [got]
        left.remove(bit)
    return parts


def finish(parts):
    return sum(p.astype(F32) for p in parts)


def on_device(
    layer_input,
    seq_lengths,
    input_gain,
    query_weight,
    key_weight,
    value_weight,
    query_gain,
    key_gain,
    output_weight,
    post_attn_gain,
    pre_ffn_gain,
    gate_weight,
    up_weight,
    down_weight,
    post_ffn_gain,
    out_cotangent,
):
    rows = layer_input.shape[0]
    dp_size = lax.axis_size("dp")
    bit_count = dp_size.bit_length() - 1
    dp_index = lax.axis_index("dp")
    head_index = lax.axis_index("head")
    core = dp_index & 1
    core_pairs = pair(dp_size, 0)
    slot_total = seq_lengths.shape[1]
    width = query_weight.shape[1]
    head_total = 2 * width // HD
    score_scale = HD ** (-0.5)

    def fetch_columns(weight):
        mine = lax.dynamic_slice_in_dim(weight, core * HD, HD, axis=1)
        first = swap_head(mine)
        second = lax.ppermute(first, "dp", core_pairs)
        return first, second

    query_first, query_second = fetch_columns(query_weight)
    output_first, output_second = fetch_columns(output_weight)

    own_ids = head_index * rows + jnp.arange(rows, dtype=jnp.int32)
    before_ids = jnp.where(head_index > 0, jnp.arange(rows, dtype=jnp.int32), -1)
    segment, position = seq_tables(seq_lengths[0], own_ids)
    before_segment, _ = seq_tables(seq_lengths[0], before_ids)
    before_segment = jnp.where(head_index > 0, before_segment, -1)
    key_ids = jnp.concatenate([before_ids, own_ids])
    key_segment = jnp.concatenate([before_segment, segment])
    visible = (key_ids[None, :] == own_ids[:, None]) | (
        (key_ids[None, :] < own_ids[:, None])
        & (key_segment[None, :] == segment[:, None])
        & (segment[:, None] < slot_total)
    )
    cosine, sine_table = angle_tables(position, HD)

    input_f32 = layer_input.astype(F32)
    normed_local, input_pull = jax.vjp(normed, input_f32, input_gain)
    normed_in = normed_local.astype(LOW)
    k_raw = dot(normed_in, key_weight)
    v_raw = dot(normed_in, value_weight)

    def query_path(raw_in, gain_vec):
        return rotary(normed(raw_in, gain_vec), cosine[:, None, :], sine_table[:, None, :])

    def key_path(raw_in, gain_vec):
        return rotary(normed(raw_in, gain_vec), cosine, sine_table)

    k_rot, key_pull = jax.vjp(key_path, k_raw, key_gain)
    kv_own = jnp.concatenate([k_rot.astype(LOW), v_raw.astype(LOW)], axis=1)
    kv_before = lax.ppermute(kv_own, "head", [(0, 1)])
    kv_all = jnp.concatenate([kv_before, kv_own], axis=0)
    k_low = kv_all[:, :HD]
    v_low = kv_all[:, HD:]

    q_raw = jnp.concatenate(
        [dot(normed_in, query_weight), dot(normed_in, query_first), dot(normed_in, query_second)],
        axis=1,
    )
    q_rot, query_pull = jax.vjp(query_path, q_raw.reshape(rows, head_total, HD), query_gain)
    q_low = q_rot.astype(LOW)

    scores = jnp.einsum("qhd,kd->hqk", q_low, k_low, preferred_element_type=F32) * score_scale
    scores = jnp.where(visible[None], scores, NEG_FILL)
    row_max = jnp.max(scores, axis=-1, keepdims=True)
    exp_scores = jnp.exp(scores - row_max)
    row_total = jnp.sum(exp_scores, axis=-1, keepdims=True)
    prob_low = (exp_scores / row_total).astype(LOW)
    log_total = row_max + jnp.log(row_total)
    attn_out = (
        jnp.einsum("hqk,kd->qhd", prob_low, v_low, preferred_element_type=F32)
        .reshape(rows, head_total * HD)
        .astype(LOW)
    )
    attn_proj = (
        row_dot(attn_out[:, :width], output_weight)
        + row_dot(attn_out[:, width : width + HD], output_first)
        + row_dot(attn_out[:, width + HD :], output_second)
    )
    attn_branch, post_attn_pull = jax.vjp(normed, attn_proj, post_attn_gain)
    hidden_state = input_f32 + attn_branch
    ffn_local, pre_ffn_pull = jax.vjp(normed, hidden_state, pre_ffn_gain)
    grad_out = out_cotangent.astype(F32)

    own_in = ffn_local.astype(LOW)
    other_in = swap_head(own_in)

    def up_part(ffn_in):
        gate_pre = dot(ffn_in, gate_weight)
        up_pre = dot(ffn_in, up_weight)
        hidden_f32 = gelu_gate(gate_pre, up_pre)
        return gate_pre.astype(LOW), up_pre.astype(LOW), hidden_f32.astype(LOW)

    own_gate, own_up, own_hidden = up_part(own_in)
    other_gate, other_up, other_hidden = up_part(other_in)
    other_proj = swap_head(row_dot(other_hidden, down_weight).astype(LOW))
    ffn_proj = row_dot(own_hidden, down_weight) + other_proj.astype(F32)
    ffn_branch, post_ffn_pull = jax.vjp(normed, ffn_proj, post_ffn_gain)
    layer_output = (hidden_state + ffn_branch).astype(LOW)
    ffn_grad_local, grad_post_ffn = post_ffn_pull(grad_out)
    own_fgrad = ffn_grad_local.astype(LOW)
    other_fgrad = swap_head(own_fgrad)

    def back_part(fgrad, gate_low, up_low):
        hidden_grad = dot(fgrad, down_weight)
        _, pull = jax.vjp(gelu_gate, gate_low.astype(F32), up_low.astype(F32))
        gate_grad, up_grad = pull(hidden_grad)
        return gate_grad.astype(LOW), up_grad.astype(LOW)

    own_ggrad, own_ugrad = back_part(own_fgrad, own_gate, own_up)
    other_ggrad, other_ugrad = back_part(other_fgrad, other_gate, other_up)
    other_zgrad = swap_head(
        (row_dot(other_ggrad, gate_weight) + row_dot(other_ugrad, up_weight)).astype(LOW)
    )
    own_zgrad = row_dot(own_ggrad, gate_weight) + row_dot(own_ugrad, up_weight)

    def weight_grad(left_own, left_other, right_own, right_other):
        left = jnp.concatenate([left_own, left_other], axis=0)
        right = jnp.concatenate([right_own, right_other], axis=0)
        return col_dot(left, right).astype(LOW)

    grad_down = weight_grad(own_fgrad, other_fgrad, own_hidden, other_hidden)
    grad_gate = weight_grad(own_in, other_in, own_ggrad, other_ggrad)
    grad_up = weight_grad(own_in, other_in, own_ugrad, other_ugrad)

    ffn_in_grad = own_zgrad + other_zgrad.astype(F32)
    state_grad_norm, grad_pre_ffn = pre_ffn_pull(ffn_in_grad)
    state_grad = grad_out + state_grad_norm
    attn_grad_local, grad_post_attn = post_attn_pull(state_grad)
    attn_grad = attn_grad_local.astype(LOW)

    heads_grad = jnp.concatenate(
        [dot(attn_grad, output_weight), dot(attn_grad, output_first), dot(attn_grad, output_second)],
        axis=1,
    )
    heads_grad = heads_grad.reshape(rows, head_total, HD).astype(LOW)
    scores = jnp.einsum("qhd,kd->hqk", q_low, k_low, preferred_element_type=F32) * score_scale
    scores = jnp.where(visible[None], scores, NEG_FILL)
    prob_f32 = jnp.exp(scores - log_total)
    prob_low = prob_f32.astype(LOW)
    prob_grad = jnp.einsum("qhd,kd->hqk", heads_grad, v_low, preferred_element_type=F32)
    row_delta = jnp.sum(prob_f32 * prob_grad, axis=-1, keepdims=True)
    score_grad = (prob_f32 * (prob_grad - row_delta)).astype(LOW)
    q_grad = jnp.einsum("hqk,kd->qhd", score_grad, k_low, preferred_element_type=F32) * score_scale
    k_grad = jnp.einsum("hqk,qhd->kd", score_grad, q_low, preferred_element_type=F32) * score_scale
    v_grad = jnp.einsum("hqk,qhd->kd", prob_low, heads_grad, preferred_element_type=F32)
    kv_grad = jnp.concatenate([k_grad, v_grad], axis=1)
    kv_back = lax.ppermute(kv_grad[:rows].astype(LOW), "head", [(1, 0)])
    kv_grad = kv_grad[rows:] + kv_back.astype(F32)
    query_raw_grad, grad_query_gain = query_pull(q_grad)
    key_raw_grad, grad_key_gain = key_pull(kv_grad[:, :HD])
    query_grad_low = query_raw_grad.reshape(rows, head_total * HD).astype(LOW)
    key_grad_low = key_raw_grad.astype(LOW)
    value_grad_low = kv_grad[:, HD:].astype(LOW)

    def in_order(two_heads):
        first, second = two_heads[:, :HD], two_heads[:, HD:]
        return jnp.where(
            core == 0,
            jnp.concatenate([first, second], axis=1),
            jnp.concatenate([second, first], axis=1),
        )

    def split_grad(left, right_heads, transposed):
        kept = right_heads[:, :width]
        sent = in_order(right_heads[:, width:])
        return col_dot(left, kept).astype(LOW), col_dot(left, sent).astype(LOW)

    output_kept, output_sent = split_grad(attn_grad, attn_out, False)
    query_kept, query_sent = split_grad(normed_in, query_grad_low, False)
    grad_kv = col_dot(normed_in, jnp.concatenate([key_grad_low, value_grad_low], axis=1)).astype(LOW)

    normed_grad = (
        row_dot(query_grad_low[:, :width], query_weight)
        + row_dot(query_grad_low[:, width : width + HD], query_first)
        + row_dot(query_grad_low[:, width + HD :], query_second)
        + row_dot(key_grad_low, key_weight)
        + row_dot(value_grad_low, value_weight)
    )
    input_grad_norm, grad_in_gain = input_pull(normed_grad)
    input_grad = (state_grad + input_grad_norm).astype(LOW)

    order = list(range(bit_count))

    def reduce_weight(grad):
        return finish(scatter_bits([grad], order, dp_size, dp_index))

    def reduce_split(kept, sent):
        return reduce_weight(kept.astype(F32) + swap_head(sent).astype(F32))

    down_part = reduce_weight(grad_down)
    gate_part = reduce_weight(grad_gate)
    up_part_out = reduce_weight(grad_up)
    output_part = reduce_split(output_kept, output_sent)
    query_part = reduce_split(query_kept, query_sent)

    gains = [grad_in_gain, grad_post_attn, grad_pre_ffn, grad_post_ffn, grad_query_gain, grad_key_gain]
    gains = [g.reshape(dp_size, -1) for g in gains]
    gain_widths = [g.shape[1] for g in gains]
    packed = jnp.concatenate(gains, axis=1)
    packed = finish(scatter_bits([packed], order, dp_size, dp_index, F32)).reshape(-1)
    kv_sum = reduce_weight(grad_kv)
    kv_sum = kv_sum + swap_head(kv_sum)
    packed = packed + swap_head(packed)
    pieces = []
    start = 0
    for gain_width in gain_widths:
        pieces.append(packed[start : start + gain_width])
        start += gain_width
    return (
        layer_output,
        input_grad,
        pieces[0],
        query_part,
        kv_sum[:, :HD],
        kv_sum[:, HD:],
        pieces[4],
        pieces[5],
        output_part,
        pieces[1],
        pieces[2],
        gate_part,
        up_part_out,
        down_part,
        pieces[3],
    )


def solution(mesh):
    placed = (
        P(("dp", "head"), None),
        P("dp", None),
        P(),
        P(None, "head"),
        P(),
        P(),
        P(),
        P(),
        P(None, "head"),
        P(),
        P(),
        P(None, "head"),
        P(None, "head"),
        P(None, "head"),
        P(),
        P(("dp", "head"), None),
    )
    return jax.shard_map(
        on_device,
        mesh=mesh,
        in_specs=placed,
        out_specs=(
            P(("dp", "head"), None),
            P(("dp", "head"), None),
            P("dp"),
            P("dp", "head"),
            P("dp", None),
            P("dp", None),
            P("dp"),
            P("dp"),
            P("dp", "head"),
            P("dp"),
            P("dp"),
            P("dp", "head"),
            P("dp", "head"),
            P("dp", "head"),
            P("dp"),
        ),
        check_vma=False,
    )
```

time: 1390 us -> 649 us (0.47)
  waiting for transfers between devices: 1010 us -> 274 us
  blocking collectives: 70.2 us -> 0 us
  starting transfers between devices: 0.66 us -> 53 us
  other arithmetic: 57.8 us -> 71.8 us
    unnamed x19 -> x0, waiting for transfers between devices: 528 us -> none
    reduce_scatter x8 -> x0, waiting for transfers between devices: 299 us -> none  [the longest x1 66.7 us: on_device(): lax.psum_scatter(grad_output, 'dp', scatter_dimension=0, tiled=True)]
    ppermute x0 -> x42, waiting for transfers between devices: none -> 274 us  [the longest x28 180 us: scatter_bits(): got = lax.ppermute(send, 'dp', pair(axis_size, bit))]
    all_gather x4 -> x0, waiting for transfers between devices: 143 us -> none  [the longest x1 36.2 us: on_device(): lax.all_gather(ffn_local.astype(jnp.bfloat16), 'head', axis=0, tiled=True)]
    unnamed x1 -> x0, blocking collectives: 61.6 us -> none
    ppermute x0 -> x42, starting transfers between devices: none -> 53 us  [the longest x28 34 us: scatter_bits(): got = lax.ppermute(send, 'dp', pair(axis_size, bit))]
    psum x1 -> x0, waiting for transfers between devices: 36.7 us -> none  [on_device(): lax.psum(grad_key.astype(jnp.bfloat16), 'head').astype(jnp.float32)]
    convert_element_type x12 -> x26, other arithmetic: 18.9 us -> 30.6 us  [the longest x18 19.3 us: scatter_bits(): send = sum((take(p, dim, 1 - mine).astype(F32) for p in parts)).astype(low)]
  transfers between devices with their start and end apart: 16 -> 42, of which waited for: 14 -> 20; matrix products, arithmetic and copies ran while one was open for 6% -> 33% of each run, Pallas kernels for 0% -> 0%
where the time goes in v1:
time: 649 us; the launch traced here: 645 us
  waiting for transfers between devices  274 us (42%)
  matrix products  199 us (31%)
  other arithmetic  71.8 us (11%)
  starting transfers between devices  53 us (8%)
  local copies, waits for them, and re-layouts  44.7 us (7%)
    ppermute x28, waiting for transfers between devices, scatter_bits(): got = lax.ppermute(send, 'dp', pair(axis_size, bit))  180 us
    ppermute x10, waiting for transfers between devices, swap_head(): return lax.ppermute(value, 'head', [(0, 1), (1, 0)])  84.7 us
    dot_general x14, matrix products, dot(): return jnp.dot(left, right, preferred_element_type=F32)  75 us
    dot_general x14, matrix products, row_dot(): return jnp.einsum('tc,dc->td', left, right, preferred_element_type=F32)  67.2 us
    dot_general x8, matrix products, col_dot(): return jnp.einsum('td,tc->dc', left, right, preferred_element_type=F32)  43.2 us
    ppermute x28, starting transfers between devices, scatter_bits(): got = lax.ppermute(send, 'dp', pair(axis_size, bit))  34 us
    convert_element_type x18, other arithmetic, scatter_bits(): send = sum((take(p, dim, 1 - mine).astype(F32) for p in parts)).astype(low)  19.3 us
    unnamed x264, local copies, waits for them, and re-layouts  15.4 us
  transfers between devices with their start and end apart: 42, of which 20 were waited for; matrix products, arithmetic and copies ran while one was open for 33% of the time, Pallas kernels for 0%

profile of v1, /device:TPU:0, one launch (start us, length us, event | category | flops | bytes accessed | tf_op | source)
XLA Modules:
  0.0 644.5 jit_solution(8508561327300221989)
XLA Ops:
  13.7 5.7 collective-permute-start
  31.7 23.7 %collective-permute-done.1 = bf16[1152,256]{1,0:T(8,128)(2,1)} collective-permute-done((bf16[1152,256]{1,0:T(8,128)(2,1)}, bf16[1152,256]{1,0:T(8,128)(2,1)}, u32[]{:S(2)}, u32[]{:S(2)}) %collective-permute-start.1) | collective-permute-done | bytes 589856 | tf_op jit(solution)/shard_map/ppermute | solution.py:68
  87.0 7.2 %fusion.211 = f32[512,3456]{1,0:T(8,128)} fusion(bf16[512,1152]{1,0:T(8,128)(2,1)S(1)} %multiply_convert_fusion, bf16[1152,3456]{1,0:T(8,128)(2,1)S(1)} %bitcast.506), kind=kOutput, calls=%fused_computation.402 | convolution fusion | flops 4076863488 | bytes 16220160 | tf_op jit(solution)/shard_map/dot_general | solution.py:56
  94.2 18.9 %collective-permute-done.5 = bf16[512,1152]{1,0:T(8,128)(2,1)S(1)} collective-permute-done((bf16[512,1152]{1,0:T(8,128)(2,1)S(1)}, bf16[512,1152]{1,0:T(8,128)(2,1)S(1)}, u32[]{:S(2)}, u32[]{:S(2)}) %collective-permute-start.5) | collective-permute-done | bytes 1179680 | tf_op jit(solution)/shard_map/ppermute | solution.py:68
  113.1 6.8 %fusion.212 = f32[512,3456]{1,0:T(8,128)} fusion(bf16[512,1152]{1,0:T(8,128)(2,1)S(1)} %collective-permute-done.5, bf16[1152,3456]{1,0:T(8,128)(2,1)S(1)} %bitcast.506), kind=kOutput, calls=%fused_computation.403 | convolution fusion | flops 4076863488 | bytes 16220160 | tf_op jit(solution)/shard_map/dot_general | solution.py:56
  120.0 11.7 %fusion.29 = (bf16[512,3456]{1,0:T(8,128)(2,1)}, bf16[512,3456]{1,0:T(8,128)(2,1)}) fusion(f32[512,3456]{1,0:T(8,128)} %fusion.212, bf16[512,1152]{1,0:T(8,128)(2,1)S(1)} %collective-permute-done.5, bf16[1152,3456]{1,0:T(8,128)(2,1)} %param.28), kind=kOutput, calls=%fused_computation.50 | convolution fusion | flops 4096327680 | bytes 23298048 | tf_op jit(solution)/shard_map/dot_general | solution.py:56
  131.7 6.9 %convolution_convert_fusion.8 = bf16[512,1152]{1,0:T(8,128)(2,1)S(1)} fusion(bf16[512,3456]{1,0:T(8,128)(2,1)} %get-tuple-element.68, bf16[1152,3456]{1,0:T(8,128)(2,1)S(1)} %bitcast.502), kind=kOutput, calls=%fused_computation.116 | convolution fusion | flops 4077453312 | bytes 12681216 | tf_op jit(solution)/shard_map/tc,dc->td/dot_general | solution.py:60
  140.4 10.8 %fusion.20 = (bf16[512,3456]{1,0:T(8,128)(2,1)}, bf16[512,3456]{1,0:T(8,128)(2,1)}) fusion(f32[512,3456]{1,0:T(8,128)S(1)} %bitcast.508, bf16[512,1152]{1,0:T(8,128)(2,1)S(1)} %multiply_convert_fusion, bf16[1152,3456]{1,0:T(8,128)(2,1)} %param.28), kind=kOutput, calls=%fused_computation.41 | convolution fusion | flops 4096327680 | bytes 23298048 | tf_op jit(solution)/shard_map/dot_general | solution.py:56
  151.3 14.8 %collective-permute-done.6 = bf16[512,1152]{1,0:T(8,128)(2,1)S(1)} collective-permute-done((bf16[512,1152]{1,0:T(8,128)(2,1)S(1)}, bf16[512,1152]{1,0:T(8,128)(2,1)S(1)}, u32[]{:S(2)}, u32[]{:S(2)}) %collective-permute-start.6) | collective-permute-done | bytes 1179680 | tf_op jit(solution)/shard_map/ppermute | solution.py:68
  166.0 7.5 %multiply_reduce_fusion.4 = (f32[512]{0:T(512)S(1)}, f32[512,1152]{1,0:T(8,128)S(1)}) fusion(bf16[512,1152]{1,0:T(8,128)(2,1)S(1)} %collective-permute-done.6, bf16[512,3456]{1,0:T(8,128)(2,1)} %get-tuple-element.66, bf16[1152,3456]{1,0:T(8,128)(2,1)S(1)} %bitcast.502), kind=kOutput, calls=%fused_computation.143 | convolution fusion | flops 4079222272 | bytes 15042560 | tf_op jit(solution)/shard_map/tc,dc->td/dot_general | solution.py:60
  177.1 4.5 fusion.73
  183.0 14.7 %fusion.36 = (bf16[512,3456]{1,0:T(8,128)(2,1)}, bf16[512,3456]{1,0:T(8,128)(2,1)}) fusion(f32[512,3456]{1,0:T(8,128)} %fusion.211, bf16[512,3456]{1,0:T(8,128)(2,1)S(1)} %copy-done.113, bf16[512,1152]{1,0:T(8,128)(2,1)S(1)} %get-tuple-element.36, bf16[1152,3456]{1,0:T(8,128)(2,1)} %param.29), kind=kOutput, calls=%fused_computation.57 | convolution fusion | flops 4124639232 | bytes 26836992 | tf_op jit(solution)/shard_map/dot_general | solution.py:56
  197.7 10.8 %fusion.213 = f32[512,1152]{1,0:T(8,128)} fusion(bf16[512,3456]{1,0:T(8,128)(2,1)} %get-tuple-element.35, bf16[1152,3456]{1,0:T(8,128)(2,1)} %param.27), kind=kOutput, calls=%fused_computation.404 | convolution fusion | flops 4076863488 | bytes 13860864 | tf_op jit(solution)/shard_map/tc,dc->td/dot_general | solution.py:60
  208.5 12.1 %fusion.43 = (bf16[512,3456]{1,0:T(8,128)(2,1)}, bf16[512,3456]{1,0:T(8,128)(2,1)}) fusion(f32[512,3456]{1,0:T(8,128)} %fusion.212, bf16[512,3456]{1,0:T(8,128)(2,1)S(1)} %copy-done.112, bf16[512,1152]{1,0:T(8,128)(2,1)S(1)} %collective-permute-done.7, bf16[1152,3456]{1,0:T(8,128)(2,1)S(1)} %bitcast.504), kind=kOutput, calls=%fused_computation.64 | convolution fusion | flops 4124639232 | bytes 26836992 | tf_op jit(solution)/shard_map/dot_general | solution.py:56
  220.6 9.4 %fusion.214 = f32[512,1152]{1,0:T(8,128)S(1)} fusion(bf16[512,3456]{1,0:T(8,128)(2,1)} %get-tuple-element.33, bf16[1152,3456]{1,0:T(8,128)(2,1)} %param.27), kind=kOutput, calls=%fused_computation.405 | convolution fusion | flops 4076863488 | bytes 13860864 | tf_op jit(solution)/shard_map/tc,dc->td/dot_general | solution.py:60
  230.0 8.4 %fusion.62 = bf16[512,1152]{1,0:T(8,128)(2,1)S(1)} fusion(f32[512,1152]{1,0:T(8,128)S(1)} %fusion.214, bf16[512,3456]{1,0:T(8,128)(2,1)S(1)} %copy-done.114, bf16[1152,3456]{1,0:T(8,128)(2,1)} %param.28), kind=kOutput, calls=%fused_computation.108 | convolution fusion | flops 4078043136 | bytes 15040512 | tf_op jit(solution)/shard_map/tc,dc->td/dot_general | solution.py:60
  239.1 11.6 %convolution_convert_fusion.2 = bf16[1152,3456]{1,0:T(8,128)(2,1)S(1)} fusion(bf16[512,3456]{1,0:T(8,128)(2,1)} %get-tuple-element.33, bf16[512,3456]{1,0:T(8,128)(2,1)} %get-tuple-element.35, bf16[512,1152]{1,0:T(8,128)(2,1)S(1)} %copy-done.110, bf16[512,1152]{1,0:T(8,128)(2,1)S(1)} %copy-done.39), kind=kOutput, calls=%fused_computation.2 | convolution fusion | flops 8176582656 | bytes 17399808 | tf_op jit(solution)/shard_map/td,tc->dc/dot_general | solution.py:64
  255.1 13.8 %convolution_convert_fusion = bf16[1152,3456]{1,0:T(8,128)(2,1)} fusion(bf16[512,3456]{1,0:T(8,128)(2,1)} %get-tuple-element.68, bf16[512,3456]{1,0:T(8,128)(2,1)} %get-tuple-element.66, bf16[512,1152]{1,0:T(8,128)(2,1)S(1)} %collective-permute-done.7, bf16[512,1152]{1,0:T(8,128)(2,1)S(1)} %get-tuple-element.36), kind=kOutput, calls=%fused_computation | convolution fusion | flops 8176582656 | bytes 17399808 | tf_op jit(solution)/shard_map/td,tc->dc/dot_general | solution.py:64
  269.0 4.6 dynamic-slice_bitcast_fusion
  274.7 11.8 %convolution_convert_fusion.1 = bf16[1152,3456]{1,0:T(8,128)(2,1)} fusion(bf16[512,3456]{1,0:T(8,128)(2,1)S(1)} %copy-done.115, bf16[512,3456]{1,0:T(8,128)(2,1)S(1)} %copy-done.111, bf16[512,1152]{1,0:T(8,128)(2,1)S(1)} %copy-done.110, bf16[512,1152]{1,0:T(8,128)(2,1)S(1)} %copy-done.39), kind=kOutput, calls=%fused_computation.1 | convolution fusion | flops 8176582656 | bytes 17399808 | tf_op jit(solution)/shard_map/td,tc->dc/dot_general | solution.py:64
  286.6 10.4 %multiply_reduce_fusion = (f32[1152]{0:T(1024)S(1)}, f32[512]{0:T(512)S(1)}, f32[512,1152]{1,0:T(8,128)S(1)}) fusion(f32[512,1152]{1,0:T(8,128)S(1)} %get-tuple-element.31, f32[512]{0:T(512)S(1)} %copy-done.86, bf16[512,1152]{1,0:T(8,128)(2,1)S(1)} %collective-permute-done.8, f32[1152]{0:T(1024)S(1)} %copy-done.74, f32[512,1152]{1,0:T(8,128)} %fusion.213, ...), kind=kOutput, calls=%fused_computation.137 | convolution fusion | flops 4082170368 | bytes 19772416 | tf_op jit(solution)/shard_map/tc,dc->td/dot_general | solution.py:60
  333.9 8.9 %collective-permute-done.9 = bf16[512,512]{0,1:T(8,128)(2,1)S(1)} collective-permute-done((bf16[512,512]{0,1:T(8,128)(2,1)S(1)}, bf16[512,512]{0,1:T(8,128)(2,1)S(1)}, u32[]{:S(2)}, u32[]{:S(2)}) %collective-permute-start.9) | collective-permute-done | bytes 524320 | tf_op jit(solution)/shard_map/ppermute | solution.py:262
  376.0 11.2 %collective-permute-done.15 = bf16[1152,512]{1,0:T(8,128)(2,1)S(1)} collective-permute-done((bf16[1152,512]{1,0:T(8,128)(2,1)S(1)}, bf16[1152,512]{1,0:T(8,128)(2,1)S(1)}, u32[]{:S(2)}, u32[]{:S(2)}) %collective-permute-start.15) | collective-permute-done | bytes 1179680 | tf_op jit(solution)/shard_map/ppermute | solution.py:68
  389.7 5.7 collective-permute-done.21
  396.0 16.1 %collective-permute-done.25 = bf16[1152,512]{1,0:T(8,128)(2,1)S(1)} collective-permute-done((bf16[1152,512]{1,0:T(8,128)(2,1)S(1)}, bf16[1152,512]{1,0:T(8,128)(2,1)S(1)}, u32[]{:S(2)}, u32[]{:S(2)}) %collective-permute-start.25) | collective-permute-done | bytes 1179680 | tf_op jit(solution)/shard_map/ppermute | solution.py:68
  460.3 25.5 %collective-permute-done.39 = bf16[2,2,72,3456]{3,2,1,0:T(8,128)(2,1)S(1)} collective-permute-done((bf16[2,2,72,3456]{3,2,1,0:T(8,128)(2,1)S(1)}, bf16[2,2,72,3456]{3,2,1,0:T(8,128)(2,1)S(1)}, u32[]{:S(2)}, u32[]{:S(2)}) %collective-permute-start.39) | collective-permute-done | bytes 1990688 | tf_op jit(solution)/shard_map/ppermute | solution.py:88
  489.0 39.4 %collective-permute-done.31 = bf16[2,2,72,3456]{3,2,1,0:T(8,128)(2,1)S(1)} collective-permute-done((bf16[2,2,72,3456]{3,2,1,0:T(8,128)(2,1)}, bf16[2,2,72,3456]{3,2,1,0:T(8,128)(2,1)S(1)}, u32[]{:S(2)}, u32[]{:S(2)}) %collective-permute-start.31) | collective-permute-done | bytes 1990688 | tf_op jit(solution)/shard_map/ppermute | solution.py:88
  531.7 38.7 %collective-permute-done.35 = bf16[2,2,72,3456]{3,2,1,0:T(8,128)(2,1)S(1)} collective-permute-done((bf16[2,2,72,3456]{3,2,1,0:T(8,128)(2,1)}, bf16[2,2,72,3456]{3,2,1,0:T(8,128)(2,1)S(1)}, u32[]{:S(2)}, u32[]{:S(2)}) %collective-permute-start.35) | collective-permute-done | bytes 1990688 | tf_op jit(solution)/shard_map/ppermute | solution.py:88
  575.4 3.3 collective-permute-start.41
  580.1 32.1 %collective-permute-done.36 = bf16[2,72,3456]{2,1,0:T(8,128)(2,1)S(1)} collective-permute-done((bf16[2,72,3456]{2,1,0:T(8,128)(2,1)S(1)}, bf16[2,72,3456]{2,1,0:T(8,128)(2,1)S(1)}, u32[]{:S(2)}, u32[]{:S(2)}) %collective-permute-start.36) | collective-permute-done | bytes 995360 | tf_op jit(solution)/shard_map/ppermute | solution.py:88
  615.8 17.9 %collective-permute-done.33 = bf16[72,3456]{1,0:T(8,128)(2,1)S(1)} collective-permute-done((bf16[72,3456]{1,0:T(8,128)(2,1)S(1)}, bf16[72,3456]{1,0:T(8,128)(2,1)S(1)}, u32[]{:S(2)}, u32[]{:S(2)}) %collective-permute-start.33) | collective-permute-done | bytes 497696 | tf_op jit(solution)/shard_map/ppermute | solution.py:88
  636.0 6.7 %collective-permute-done.37 = bf16[72,3456]{1,0:T(8,128)(2,1)S(1)} collective-permute-done((bf16[72,3456]{1,0:T(8,128)(2,1)S(1)}, bf16[72,3456]{1,0:T(8,128)(2,1)S(1)}, u32[]{:S(2)}, u32[]{:S(2)}) %collective-permute-start.37) | collective-permute-done | bytes 497696 | tf_op jit(solution)/shard_map/ppermute | solution.py:88
  (479 shorter events, 210.0 us)
Async XLA Ops:
  13.7 42.9 %collective-permute-start = (bf16[512,512]{0,1:T(8,128)(2,1)}, bf16[512,512]{0,1:T(8,128)(2,1)}, u32[]{:S(2)}, u32[]{:S(2)}) collective-permute-start(bf16[512,512]{0,1:T(8,128)(2,1)} %pad_maximum_fusion.9), channel_id=1, source_target_pairs={{0,1},{2,3},{4,5},{6,7},{8,9},{10,11},{12,13},{14,15},{16,17},{18,... | collective-permute-start | bytes 1572872 | tf_op jit(solution)/shard_map/ppermute | solution.py:165
  20.3 38.6 %collective-permute-start.3 = (bf16[1152,256]{1,0:T(8,128)(2,1)}, bf16[1152,256]{1,0:T(8,128)(2,1)}, u32[]{:S(2)}, u32[]{:S(2)}) collective-permute-start(bf16[1152,256]{1,0:T(8,128)(2,1)} %constant_dynamic-slice_fusion.14), channel_id=1, source_target_pairs={{0,1},{1,0},{2,3},{3,2},{4,5},{5,4},{6,7},{7,6},{8,9},{9,8},{10,11... | collective-permute-start | bytes 1769480 | tf_op jit(solution)/shard_map/ppermute | solution.py:68
  21.1 34.2 %collective-permute-start.1 = (bf16[1152,256]{1,0:T(8,128)(2,1)}, bf16[1152,256]{1,0:T(8,128)(2,1)}, u32[]{:S(2)}, u32[]{:S(2)}) collective-permute-start(bf16[1152,256]{1,0:T(8,128)(2,1)} %constant_dynamic-slice_fusion.15), channel_id=1, source_target_pairs={{0,1},{1,0},{2,3},{3,2},{4,5},{5,4},{6,7},{7,6},{8,9},{9,8},{10,11... | collective-permute-start | bytes 1769480 | tf_op jit(solution)/shard_map/ppermute | solution.py:68
  58.9 21.7 %collective-permute-start.4 = (bf16[1152,256]{1,0:T(8,128)(2,1)}, bf16[1152,256]{1,0:T(8,128)(2,1)}, u32[]{:S(2)}, u32[]{:S(2)}) collective-permute-start(bf16[1152,256]{1,0:T(8,128)(2,1)} %collective-permute-done.3), channel_id=1, source_target_pairs={{0,2},{2,0},{4,6},{6,4},{8,10},{10,8},{12,14},{14,12},{16,18},{18,... | collective-permute-start | bytes 1769480 | tf_op jit(solution)/shard_map/ppermute | solution.py:131
  84.5 28.6 %collective-permute-start.5 = (bf16[512,1152]{1,0:T(8,128)(2,1)S(1)}, bf16[512,1152]{1,0:T(8,128)(2,1)S(1)}, u32[]{:S(2)}, u32[]{:S(2)}) collective-permute-start(bf16[512,1152]{1,0:T(8,128)(2,1)S(1)} %multiply_convert_fusion), channel_id=1, source_target_pairs={{0,1},{1,0},{2,3},{3,2},{4,5},{5,4},{6,7},{7,6},{8,9},{9,8},{10,11... | collective-permute-start | bytes 3538952 | tf_op jit(solution)/shard_map/ppermute | solution.py:68
  138.6 27.4 %collective-permute-start.6 = (bf16[512,1152]{1,0:T(8,128)(2,1)S(1)}, bf16[512,1152]{1,0:T(8,128)(2,1)S(1)}, u32[]{:S(2)}, u32[]{:S(2)}) collective-permute-start(bf16[512,1152]{1,0:T(8,128)(2,1)S(1)} %convolution_convert_fusion.8), channel_id=1, source_target_pairs={{0,1},{1,0},{2,3},{3,2},{4,5},{5,4},{6,7},{7,6},{8,9},{9,8},{10,11... | collective-permute-start | bytes 3538952 | tf_op jit(solution)/shard_map/ppermute | solution.py:68
  181.6 26.8 %collective-permute-start.7 = (bf16[512,1152]{1,0:T(8,128)(2,1)S(1)}, bf16[512,1152]{1,0:T(8,128)(2,1)S(1)}, u32[]{:S(2)}, u32[]{:S(2)}) collective-permute-start(bf16[512,1152]{1,0:T(8,128)(2,1)S(1)} %get-tuple-element.36), channel_id=1, source_target_pairs={{0,1},{1,0},{2,3},{3,2},{4,5},{5,4},{6,7},{7,6},{8,9},{9,8},{10,11... | collective-permute-start | bytes 3538952 | tf_op jit(solution)/shard_map/ppermute | solution.py:68
  238.4 48.2 %collective-permute-start.8 = (bf16[512,1152]{1,0:T(8,128)(2,1)S(1)}, bf16[512,1152]{1,0:T(8,128)(2,1)S(1)}, u32[]{:S(2)}, u32[]{:S(2)}) collective-permute-start(bf16[512,1152]{1,0:T(8,128)(2,1)S(1)} %fusion.62), channel_id=1, source_target_pairs={{0,1},{1,0},{2,3},{3,2},{4,5},{5,4},{6,7},{7,6},{8,9},{9,8},{10,11... | collective-permute-start | bytes 3538952 | tf_op jit(solution)/shard_map/ppermute | solution.py:68
  273.5 156.1 %collective-permute-start.38 = (bf16[2,2,2,72,3456]{4,3,2,1,0:T(8,128)(2,1)}, bf16[2,2,2,72,3456]{4,3,2,1,0:T(8,128)(2,1)}, u32[]{:S(2)}, u32[]{:S(2)}) collective-permute-start(bf16[2,2,2,72,3456]{4,3,2,1,0:T(8,128)(2,1)} %dynamic-slice_bitcast_fusion), channel_id=1, source_target_pairs={{0,2},{2,0},{4,6},{6,4},{8,10},{10,8},{12,14},{14,12},{16,18},{18,... | collective-permute-start | bytes 11943944 | tf_op jit(solution)/shard_map/ppermute | solution.py:88
  273.5 158.8 %collective-permute-start.30 = (bf16[2,2,2,72,3456]{4,3,2,1,0:T(8,128)(2,1)}, bf16[2,2,2,72,3456]{4,3,2,1,0:T(8,128)(2,1)}, u32[]{:S(2)}, u32[]{:S(2)}) collective-permute-start(bf16[2,2,2,72,3456]{4,3,2,1,0:T(8,128)(2,1)} %dynamic-slice_bitcast_fusion.2), channel_id=1, source_target_pairs={{0,2},{2,0},{4,6},{6,4},{8,10},{10,8},{12,14},{14,12},{16,18},{18,... | collective-permute-start | bytes 11943944 | tf_op jit(solution)/shard_map/ppermute | solution.py:88
  327.6 15.2 %collective-permute-start.9 = (bf16[512,512]{0,1:T(8,128)(2,1)S(1)}, bf16[512,512]{0,1:T(8,128)(2,1)S(1)}, u32[]{:S(2)}, u32[]{:S(2)}) collective-permute-start(bf16[512,512]{0,1:T(8,128)(2,1)S(1)} %fusion.93), channel_id=1, source_target_pairs={{1,0},{3,2},{5,4},{7,6},{9,8},{11,10},{13,12},{15,14},{17,16},{19,... | collective-permute-start | bytes 1572872 | tf_op jit(solution)/shard_map/ppermute | solution.py:262
  358.4 28.8 %collective-permute-start.15 = (bf16[1152,512]{1,0:T(8,128)(2,1)S(1)}, bf16[1152,512]{1,0:T(8,128)(2,1)S(1)}, u32[]{:S(2)}, u32[]{:S(2)}) collective-permute-start(bf16[1152,512]{1,0:T(8,128)(2,1)S(1)} %convolution_convert_fusion.6), channel_id=1, source_target_pairs={{0,1},{1,0},{2,3},{3,2},{4,5},{5,4},{6,7},{7,6},{8,9},{9,8},{10,11... | collective-permute-start | bytes 3538952 | tf_op jit(solution)/shard_map/ppermute | solution.py:68
  365.0 10.8 %collective-permute-start.20 = (bf16[2,2,2,72,512]{4,3,2,1,0:T(8,128)(2,1)S(1)}, bf16[2,2,2,72,512]{4,3,2,1,0:T(8,128)(2,1)S(1)}, u32[]{:S(2)}, u32[]{:S(2)}) collective-permute-start(bf16[2,2,2,72,512]{4,3,2,1,0:T(8,128)(2,1)S(1)} %dynamic-slice_bitcast_fusion.3), channel_id=1, source_target_pairs={{0,2},{2,0},{4,6},{6,4},{8,10},{10,8},{12,14},{14,12},{16,18},{18,... | collective-permute-start | bytes 1769480 | tf_op jit(solution)/shard_map/ppermute | solution.py:88
  371.5 40.6 %collective-permute-start.25 = (bf16[1152,512]{1,0:T(8,128)(2,1)S(1)}, bf16[1152,512]{1,0:T(8,128)(2,1)S(1)}, u32[]{:S(2)}, u32[]{:S(2)}) collective-permute-start(bf16[1152,512]{1,0:T(8,128)(2,1)S(1)} %convolution_convert_fusion.3), channel_id=1, source_target_pairs={{0,1},{1,0},{2,3},{3,2},{4,5},{5,4},{6,7},{7,6},{8,9},{9,8},{10,11... | collective-permute-start | bytes 3538952 | tf_op jit(solution)/shard_map/ppermute | solution.py:68
  375.8 61.4 %collective-permute-start.34 = (bf16[2,2,2,72,3456]{4,3,2,1,0:T(8,128)(2,1)}, bf16[2,2,2,72,3456]{4,3,2,1,0:T(8,128)(2,1)S(1)}, u32[]{:S(2)}, u32[]{:S(2)}) collective-permute-start(bf16[2,2,2,72,3456]{4,3,2,1,0:T(8,128)(2,1)} %dynamic-slice_bitcast_fusion.1), channel_id=1, source_target_pairs={{0,2},{2,0},{4,6},{6,4},{8,10},{10,8},{12,14},{14,12},{16,18},{18,... | collective-permute-start | bytes 11943944 | tf_op jit(solution)/shard_map/ppermute | solution.py:88
  387.2 8.2 %collective-permute-start.21 = (bf16[2,2,72,512]{3,2,1,0:T(8,128)(2,1)S(1)}, bf16[2,2,72,512]{3,2,1,0:T(8,128)(2,1)S(1)}, u32[]{:S(2)}, u32[]{:S(2)}) collective-permute-start(bf16[2,2,72,512]{3,2,1,0:T(8,128)(2,1)S(1)} %fusion.103), channel_id=1, source_target_pairs={{0,4},{2,6},{4,0},{6,2},{8,12},{10,14},{12,8},{14,10},{16,20},{18,... | collective-permute-start | bytes 884744 | tf_op jit(solution)/shard_map/ppermute | solution.py:88
  395.4 24.9 %collective-permute-start.14 = (f32[320]{0:T(512)S(1)}, f32[320]{0:T(512)S(1)}, u32[]{:S(2)}, u32[]{:S(2)}) collective-permute-start(f32[320]{0:T(512)S(1)} %add_reduce_fusion), channel_id=1, source_target_pairs={{0,1},{1,0},{2,3},{3,2},{4,5},{5,4},{6,7},{7,6},{8,9},{9,8},{10,11... | collective-permute-start | bytes 3848 | tf_op jit(solution)/shard_map/ppermute | solution.py:68
  426.2 13.6 %collective-permute-start.24 = (f32[72,512]{1,0:T(8,128)S(1)}, f32[72,512]{1,0:T(8,128)S(1)}, u32[]{:S(2)}, u32[]{:S(2)}) collective-permute-start(f32[72,512]{1,0:T(8,128)S(1)} %fusion.148), channel_id=1, source_target_pairs={{0,1},{1,0},{2,3},{3,2},{4,5},{5,4},{6,7},{7,6},{8,9},{9,8},{10,11... | collective-permute-start | bytes 442376 | tf_op jit(solution)/shard_map/ppermute | solution.py:68
  426.9 16.0 %collective-permute-start.27 = (bf16[2,2,72,512]{3,2,1,0:T(8,128)(2,1)S(1)}, bf16[2,2,72,512]{3,2,1,0:T(8,128)(2,1)}, u32[]{:S(2)}, u32[]{:S(2)}) collective-permute-start(bf16[2,2,72,512]{3,2,1,0:T(8,128)(2,1)S(1)} %fusion.102), channel_id=1, source_target_pairs={{0,4},{2,6},{4,0},{6,2},{8,12},{10,14},{12,8},{14,10},{16,20},{18,... | collective-permute-start | bytes 884744 | tf_op jit(solution)/shard_map/ppermute | solution.py:88
  429.6 15.9 %collective-permute-start.17 = (bf16[2,2,72,512]{3,2,1,0:T(8,128)(2,1)S(1)}, bf16[2,2,72,512]{3,2,1,0:T(8,128)(2,1)S(1)}, u32[]{:S(2)}, u32[]{:S(2)}) collective-permute-start(bf16[2,2,72,512]{3,2,1,0:T(8,128)(2,1)S(1)} %fusion.104), channel_id=1, source_target_pairs={{0,4},{2,6},{4,0},{6,2},{8,12},{10,14},{12,8},{14,10},{16,20},{18,... | collective-permute-start | bytes 884744 | tf_op jit(solution)/shard_map/ppermute | solution.py:88
  432.3 53.5 %collective-permute-start.39 = (bf16[2,2,72,3456]{3,2,1,0:T(8,128)(2,1)S(1)}, bf16[2,2,72,3456]{3,2,1,0:T(8,128)(2,1)S(1)}, u32[]{:S(2)}, u32[]{:S(2)}) collective-permute-start(bf16[2,2,72,3456]{3,2,1,0:T(8,128)(2,1)S(1)} %fusion.58), channel_id=1, source_target_pairs={{0,4},{2,6},{4,0},{6,2},{8,12},{10,14},{12,8},{14,10},{16,20},{18,... | collective-permute-start | bytes 5971976 | tf_op jit(solution)/shard_map/ppermute | solution.py:88
  437.2 91.2 %collective-permute-start.31 = (bf16[2,2,72,3456]{3,2,1,0:T(8,128)(2,1)}, bf16[2,2,72,3456]{3,2,1,0:T(8,128)(2,1)S(1)}, u32[]{:S(2)}, u32[]{:S(2)}) collective-permute-start(bf16[2,2,72,3456]{3,2,1,0:T(8,128)(2,1)} %fusion.60), channel_id=1, source_target_pairs={{0,4},{2,6},{4,0},{6,2},{8,12},{10,14},{12,8},{14,10},{16,20},{18,... | collective-permute-start | bytes 5971976 | tf_op jit(solution)/shard_map/ppermute | solution.py:88
  439.8 130.6 %collective-permute-start.35 = (bf16[2,2,72,3456]{3,2,1,0:T(8,128)(2,1)}, bf16[2,2,72,3456]{3,2,1,0:T(8,128)(2,1)S(1)}, u32[]{:S(2)}, u32[]{:S(2)}) collective-permute-start(bf16[2,2,72,3456]{3,2,1,0:T(8,128)(2,1)} %fusion.59), channel_id=1, source_target_pairs={{0,4},{2,6},{4,0},{6,2},{8,12},{10,14},{12,8},{14,10},{16,20},{18,... | collective-permute-start | bytes 5971976 | tf_op jit(solution)/shard_map/ppermute | solution.py:88
  446.6 7.4 %collective-permute-start.18 = (bf16[2,72,512]{2,1,0:T(8,128)(2,1)S(1)}, bf16[2,72,512]{2,1,0:T(8,128)(2,1)S(1)}, u32[]{:S(2)}, u32[]{:S(2)}) collective-permute-start(bf16[2,72,512]{2,1,0:T(8,128)(2,1)S(1)} %fusion.138), channel_id=1, source_target_pairs={{0,8},{2,10},{4,12},{6,14},{8,0},{10,2},{12,4},{14,6},{16,24},{18,... | collective-permute-start | bytes 442376 | tf_op jit(solution)/shard_map/ppermute | solution.py:88
  451.4 7.3 %collective-permute-start.29 = (bf16[72,512]{1,0:T(8,128)(2,1)S(1)}, bf16[72,512]{1,0:T(8,128)(2,1)S(1)}, u32[]{:S(2)}, u32[]{:S(2)}) collective-permute-start(bf16[72,512]{1,0:T(8,128)(2,1)S(1)} %fusion.145), channel_id=1, source_target_pairs={{0,16},{2,18},{4,20},{6,22},{8,24},{10,26},{12,28},{14,30},{16,0},... | collective-permute-start | bytes 221192 | tf_op jit(solution)/shard_map/ppermute | solution.py:88
  454.9 117.6 %collective-permute-start.19 = (bf16[72,512]{1,0:T(8,128)(2,1)S(1)}, bf16[72,512]{1,0:T(8,128)(2,1)S(1)}, u32[]{:S(2)}, u32[]{:S(2)}) collective-permute-start(bf16[72,512]{1,0:T(8,128)(2,1)S(1)} %fusion.149), channel_id=1, source_target_pairs={{0,16},{2,18},{4,20},{6,22},{8,24},{10,26},{12,28},{14,30},{16,0},... | collective-permute-start | bytes 221192 | tf_op jit(solution)/shard_map/ppermute | solution.py:88
  487.4 86.7 %collective-permute-start.40 = (bf16[2,72,3456]{2,1,0:T(8,128)(2,1)S(1)}, bf16[2,72,3456]{2,1,0:T(8,128)(2,1)S(1)}, u32[]{:S(2)}, u32[]{:S(2)}) collective-permute-start(bf16[2,72,3456]{2,1,0:T(8,128)(2,1)S(1)} %fusion.83), channel_id=1, source_target_pairs={{0,8},{2,10},{4,12},{6,14},{8,0},{10,2},{12,4},{14,6},{16,24},{18,... | collective-permute-start | bytes 2985992 | tf_op jit(solution)/shard_map/ppermute | solution.py:88
  530.0 48.7 %collective-permute-start.32 = (bf16[2,72,3456]{2,1,0:T(8,128)(2,1)S(1)}, bf16[2,72,3456]{2,1,0:T(8,128)(2,1)S(1)}, u32[]{:S(2)}, u32[]{:S(2)}) collective-permute-start(bf16[2,72,3456]{2,1,0:T(8,128)(2,1)S(1)} %fusion.85), channel_id=1, source_target_pairs={{0,8},{2,10},{4,12},{6,14},{8,0},{10,2},{12,4},{14,6},{16,24},{18,... | collective-permute-start | bytes 2985992 | tf_op jit(solution)/shard_map/ppermute | solution.py:88
  570.8 41.5 %collective-permute-start.36 = (bf16[2,72,3456]{2,1,0:T(8,128)(2,1)S(1)}, bf16[2,72,3456]{2,1,0:T(8,128)(2,1)S(1)}, u32[]{:S(2)}, u32[]{:S(2)}) collective-permute-start(bf16[2,72,3456]{2,1,0:T(8,128)(2,1)S(1)} %fusion.84), channel_id=1, source_target_pairs={{0,8},{2,10},{4,12},{6,14},{8,0},{10,2},{12,4},{14,6},{16,24},{18,... | collective-permute-start | bytes 2985992 | tf_op jit(solution)/shard_map/ppermute | solution.py:88
  575.4 38.1 %collective-permute-start.41 = (bf16[72,3456]{1,0:T(8,128)(2,1)S(1)}, bf16[72,3456]{1,0:T(8,128)(2,1)S(1)}, u32[]{:S(2)}, u32[]{:S(2)}) collective-permute-start(bf16[72,3456]{1,0:T(8,128)(2,1)S(1)} %fusion.94), channel_id=1, source_target_pairs={{0,16},{2,18},{4,20},{6,22},{8,24},{10,26},{12,28},{14,30},{16,0},... | collective-permute-start | bytes 1493000 | tf_op jit(solution)/shard_map/ppermute | solution.py:88
  580.0 53.6 %collective-permute-start.33 = (bf16[72,3456]{1,0:T(8,128)(2,1)S(1)}, bf16[72,3456]{1,0:T(8,128)(2,1)S(1)}, u32[]{:S(2)}, u32[]{:S(2)}) collective-permute-start(bf16[72,3456]{1,0:T(8,128)(2,1)S(1)} %fusion.98), channel_id=1, source_target_pairs={{0,16},{2,18},{4,20},{6,22},{8,24},{10,26},{12,28},{14,30},{16,0},... | collective-permute-start | bytes 1493000 | tf_op jit(solution)/shard_map/ppermute | solution.py:88
  612.6 30.2 %collective-permute-start.37 = (bf16[72,3456]{1,0:T(8,128)(2,1)S(1)}, bf16[72,3456]{1,0:T(8,128)(2,1)S(1)}, u32[]{:S(2)}, u32[]{:S(2)}) collective-permute-start(bf16[72,3456]{1,0:T(8,128)(2,1)S(1)} %fusion.96), channel_id=1, source_target_pairs={{0,16},{2,18},{4,20},{6,22},{8,24},{10,26},{12,28},{14,30},{16,0},... | collective-permute-start | bytes 1493000 | tf_op jit(solution)/shard_map/ppermute | solution.py:88
  (142 other events, 1150.4 us)
